TPU v7x, 128 devices: a whole 4x4x4 slice. The times are simulated.
128 devices in a mesh: row: 8 (over y, core), col: 16 (over x, z).
Axes of the slice: x: 4, y: 4, z: 4, core: 2. Of those that a mesh axis runs over, the one named last changes fastest.
Arguments:
- user_emb: float32 [8, 16, 2048, 128], P('row', 'col'), may hold values from -2.4 to 2.4
- item_emb: float32 [16, 8, 1024, 128], P('col', 'row'), may hold values from -2.4 to 2.4
- tile_vals: bfloat16 [8, 16, 512, 128, 128], P('row', 'col'), may hold values from 0 to 0.029907227
- tile_rows: int32 [8, 16, 512], P('row', 'col'), may hold values from 0 to 255
- tile_cols: int32 [8, 16, 512], P('row', 'col'), may hold values from 0 to 63
- tile_count: int32 [8, 16], P('row', 'col'), may hold values from 128 to 512, as said below
- pair_users: int32 [65536], P(('row', 'col')), may hold values from 0 to 262143, as said below
- pair_items: int32 [65536], P(('row', 'col')), may hold values from 0 to 131071, as said below
- negatives: int32 [1024], replicated, may hold values from 0 to 131071, as said below
Outputs:
- user_final: float32 [8, 16, 2048, 128], P('row', 'col')
- item_final: float32 [16, 8, 1024, 128], P('col', 'row')
- bpr_terms: float32 [65536, 1024], P(('row', 'col'))
Inputs may be any that keep to these rules, and one draw needn't show every extreme that they name: `pair_users`: taken in aligned blocks of 512 entries, at most 8 entries of one block name users that one device holds in user_emb; in every draw some device's users are named exactly 8 times in every block. `pair_items`: taken in aligned blocks of 512 entries, at most 8 entries of one block name items that one device holds in item_emb; in every draw some device's items are named exactly 8 times in every block. `tile_count`: some block has all 512 slots live. `negatives`: entry j names an item that the device with row index (j // 8) // 16 and col index (j // 8) % 16 holds in item_emb.
All inputs are finite; a program needn't handle non-finite values.
Results may differ from a plain program's by a relative error of at most 0.009.
Values may be sent and summed in bfloat16 or wider, within the bound.
A program may use at most 128 MiB of HBM per device.

v0:
```python
import math
import jax
import jax.numpy as jnp
from jax import lax
from jax.sharding import Mesh
from jax.sharding import PartitionSpec as P

ROW = ("row_0", "row_1")
COL = ("col_0", "col_1")
ROW_COL = ("row_0", "row_1", "col_0", "col_1")


def from_everyone(array, axis):
    copies = jnp.broadcast_to(array, (lax.axis_size(axis), *array.shape))
    return lax.all_to_all(copies, axis, split_axis=0, concat_axis=0, tiled=True)


def in_order(blocks, dim):
    blocks = jnp.moveaxis(blocks, 0, dim)
    shape = blocks.shape
    return blocks.reshape(*shape[:dim], shape[dim] * shape[dim + 1], *shape[dim + 2 :])


def collect(array, axis, dim):
    blocks = from_everyone(array, axis)
    return in_order(blocks, dim)


def in_blocks(array, dim, length):
    shape = array.shape
    blocks = array.reshape(*shape[:dim], length, shape[dim] // length, *shape[dim + 1 :])
    return jnp.moveaxis(blocks, dim, 0)


def sent_and_summed(array, axis, dim):
    blocks = in_blocks(array, dim, lax.axis_size(axis))
    arrived = lax.all_to_all(blocks, axis, split_axis=0, concat_axis=0, tiled=True)
    return arrived.astype(jnp.float32).sum(axis=0)


def gather_in_order(array, axes, sequence):
    blocks = array[None]
    for k in sequence:
        blocks = lax.all_gather(blocks, axes[k], axis=0, tiled=True)
    held = [lax.axis_size(axes[k]) for k in reversed(sequence)]
    blocks = blocks.reshape(*held, *array.shape)
    turned = sorted(range(len(sequence)), key=lambda place: sequence[len(sequence) - 1 - place])
    return blocks.transpose(*turned, *range(len(sequence), blocks.ndim)).reshape(-1, *array.shape)


def whole_of(array, axes, sequence, dim):
    return in_order(gather_in_order(array, axes, sequence), dim)


def tile_products(values_all, row_all, col_all, number, user_tiles, item_tiles):
    total = values_all.shape[0]
    width = math.gcd(total, 64)
    blocks = (number + width - 1) // width

    def advance(block_index, totals):
        user_part, item_part = totals
        offset = block_index * width
        values = lax.dynamic_slice_in_dim(values_all, offset, width, 0)
        row_ids = lax.dynamic_slice_in_dim(row_all, offset, width, 0)
        col_ids = lax.dynamic_slice_in_dim(col_all, offset, width, 0)
        live_mask = (offset + jnp.arange(width, dtype=jnp.int32) < number).astype(jnp.float32)[
            :, None, None
        ]
        to_users = (
            jnp.einsum(
                "tij,tje->tie", values, item_tiles[col_ids], preferred_element_type=jnp.float32
            )
            * live_mask
        )
        to_items = (
            jnp.einsum(
                "tij,tie->tje", values, user_tiles[row_ids], preferred_element_type=jnp.float32
            )
            * live_mask
        )
        return (user_part.at[row_ids].add(to_users), item_part.at[col_ids].add(to_items))

    start = (jnp.zeros(user_tiles.shape, jnp.float32), jnp.zeros(item_tiles.shape, jnp.float32))
    return lax.fori_loop(0, blocks, advance, start)


def place_requests(owner, local, devices, slots_per):
    hits = (owner[:, None] == jnp.arange(devices, dtype=jnp.int32)[None, :]).astype(jnp.int32)
    rank = jnp.sum((jnp.cumsum(hits, axis=0) - 1) * hits, axis=1)
    slot = owner * slots_per + rank
    request = jnp.zeros((devices * slots_per,), jnp.int32).at[slot].set(local)
    return (slot, request.reshape(devices, slots_per))


def on_device(
    user_emb,
    item_emb,
    tile_vals,
    tile_rows,
    tile_cols,
    tile_count,
    pair_users,
    pair_items,
    negatives,
):
    row_count = lax.axis_size(ROW)
    col_count = lax.axis_size(COL)
    user_dev = user_emb.shape[2]
    item_dev = item_emb.shape[2]
    embed = user_emb.shape[3]
    tile_side = tile_vals.shape[-1]
    user_whole = lax.all_gather(user_emb.astype(jnp.bfloat16), COL, axis=1, tiled=True)
    item_whole = collect(item_emb.astype(jnp.bfloat16), ROW, 1)
    user_tiles = user_whole.reshape(-1, tile_side, embed)
    item_tiles = item_whole.reshape(-1, tile_side, embed)
    user_part, item_part = tile_products(
        tile_vals[0, 0], tile_rows[0, 0], tile_cols[0, 0], tile_count[0, 0], user_tiles, item_tiles
    )
    user_prop = lax.psum_scatter(
        user_part.reshape(-1, embed).astype(jnp.bfloat16), COL, scatter_dimension=0, tiled=True
    ).astype(jnp.float32)
    item_prop = sent_and_summed(item_part.reshape(-1, embed).astype(jnp.bfloat16), ROW, 0)
    user_final = (user_emb[0, 0] + user_prop) * 0.5
    item_final = (item_emb[0, 0] + item_prop) * 0.5
    devices = row_count * col_count
    slots_per = 2 * pair_users.shape[0] // devices
    user_owner = pair_users // user_dev
    user_local = pair_users % user_dev
    item_holder = pair_items // item_dev
    item_owner = item_holder % row_count * col_count + item_holder // row_count
    item_local = pair_items % item_dev
    user_slot, user_request = place_requests(user_owner, user_local, devices, slots_per)
    item_slot, item_request = place_requests(item_owner, item_local, devices, slots_per)
    user_wanted = lax.all_to_all(user_request, ROW_COL, split_axis=0, concat_axis=0, tiled=True)
    item_wanted = lax.all_to_all(item_request, ROW_COL, split_axis=0, concat_axis=0, tiled=True)
    user_rows = lax.all_to_all(
        user_final[user_wanted].astype(jnp.bfloat16),
        ROW_COL,
        split_axis=0,
        concat_axis=0,
        tiled=True,
    ).astype(jnp.float32)
    item_rows = lax.all_to_all(
        item_final[item_wanted].astype(jnp.bfloat16),
        ROW_COL,
        split_axis=0,
        concat_axis=0,
        tiled=True,
    ).astype(jnp.float32)
    user_vec = user_rows.reshape(-1, embed)[user_slot]
    item_vec = item_rows.reshape(-1, embed)[item_slot]
    offset = (lax.axis_index(COL) * row_count + lax.axis_index(ROW)) * item_dev
    neg_each = negatives.shape[0] // devices
    device_rank = lax.axis_index(ROW) * col_count + lax.axis_index(COL)
    mine = lax.dynamic_slice_in_dim(negatives, device_rank * neg_each, neg_each, 0) - offset
    negative_vec = whole_of(item_final[mine], ROW_COL, (0, 2, 3, 1), 0)
    positive = jnp.sum(user_vec * item_vec, axis=1)
    against = jnp.dot(user_vec, negative_vec.T, precision=lax.Precision.HIGHEST)
    bpr_terms = jnp.log1p(jnp.exp(against - positive[:, None]))
    return (user_final.reshape(user_emb.shape), item_final.reshape(item_emb.shape), bpr_terms)


def solution(mesh):
    torus = Mesh(mesh.devices.reshape(4, 2, 4, 4), ("row_0", "row_1", "col_0", "col_1"))
    return jax.shard_map(
        on_device,
        mesh=torus,
        in_specs=(
            P(ROW, COL, None, None),
            P(COL, ROW, None, None),
            P(ROW, COL, None, None, None),
            P(ROW, COL, None),
            P(ROW, COL, None),
            P(ROW, COL),
            P(ROW_COL),
            P(ROW_COL),
            P(),
        ),
        out_specs=(P(ROW, COL, None, None), P(COL, ROW, None, None), P(ROW_COL, None)),
        check_vma=False,
    )
```

profile of v0, /device:TPU:1, one launch (start us, length us, event | category | flops | bytes accessed | tf_op | source)
XLA Modules:
  0.0 615.4 jit_solution(11518100190499439016)
XLA Ops:
  7.2 2.1 bitcast_convert_fusion
  9.3 1.1 convert_bitcast_fusion.2
  10.4 1.6 broadcast_in_dim.25
  12.0 6.0 all-to-all-start
  18.6 25.5 %all-to-all-done = bf16[8,1,1,1024,128]{4,3,2,1,0:T(8,128)(2,1)S(1)} async-done(((bf16[8,1,1,1024,128]{4,3,2,1,0:T(8,128)(2,1)}), bf16[8,1,1,1024,128]{4,3,2,1,0:T(8,128)(2,1)S(1)}, u32[]{:S(2)}, u32[]{:S(2)}) %all-to-all-start) | async-done | bytes 2097184 | tf_op jit(solution)/shard_map/all_to_all | solution.py:15
  44.1 40.6 %all-gather.3.cloned.1.call-done = bf16[1,16,2048,128]{3,2,0,1:T(8,128)(2,1)} async-done(((bf16[1,1,2048,128]{3,2,0,1:T(8,128)(2,1)}), bf16[1,16,2048,128]{3,2,0,1:T(8,128)(2,1)}) %all-gather.3.cloned.1.call-update) | async-done | bytes 8388624 | tf_op jit(solution)/shard_map/all_gather | solution.py:112
  84.7 7.8 %broadcast_in_dim.23 = f32[256,128,128]{2,1,0:T(8,128)} broadcast(f32[]{:T(128)} %constant.123.clone.1), dimensions={} | broadcast | bytes 16777220 | tf_op jit(solution)/shard_map/broadcast_in_dim | solution.py:83
  92.5 2.5 broadcast_in_dim.24
  95.0 135.0 %while.12 = (s32[]{:T(128)}, f32[256,128,128]{2,1,0:T(8,128)}, f32[64,128,128]{2,1,0:T(8,128)}, s32[]{:T(128)}, s32[512]{0:T(512)}, /*index=5*/bf16[512,128,128]...) while((s32[]{:T(128)}, f32[256,128,128]{2,1,0:T(8,128)}, ...), condition=%wide.region_3.4_spmd, body=%wide.region_0.3_spmd.sunk | while | flops 541067840 | bytes 67120640 | solution.py:84
  95.0 0.8 compare_select_fusion.8
  96.3 2.5 gather_fusion
  98.9 0.7 compare_convert_fusion.2
  99.5 4.2 convolution_multiply_fusion.4
  103.8 13.7 %scatter_fusion = f32[256,128,128]{2,1,0:T(8,128)} fusion(f32[256,128,128]{2,1,0:T(8,128)} %get-tuple-element.166, s32[64]{0:T(128)S(1)} %get-tuple-element.149, f32[64,128,128]{2,1,0:T(8,128)} %convolution_multiply_fusion.4), kind=kCustom, calls=%fused_computation.8.clone.1 | custom fusion | flops 1048576 | bytes 12583168 | tf_op jit(solution)/shard_map/while/body/scatter-add | solution.py:81
  117.5 4.3 gather_fusion.1
  121.9 4.6 convolution_multiply_fusion.5
  126.5 13.6 %scatter_fusion.1 = f32[64,128,128]{2,1,0:T(8,128)} fusion(f32[64,128,128]{2,1,0:T(8,128)} %get-tuple-element.167, s32[64]{0:T(128)S(1)} %get-tuple-element.150, f32[64,128,128]{2,1,0:T(8,128)} %convolution_multiply_fusion.5), kind=kCustom, calls=%fused_computation.9.clone.1 | custom fusion | flops 1048576 | bytes 12583168 | tf_op jit(solution)/shard_map/while/body/scatter-add | solution.py:81
  140.0 0.8 compare_select_fusion.8
  140.9 0.5 copy-done
  141.4 2.5 gather_fusion
  143.9 0.7 compare_convert_fusion.2
  144.6 4.2 convolution_multiply_fusion.4
  148.8 13.6 %scatter_fusion = f32[256,128,128]{2,1,0:T(8,128)} fusion(f32[256,128,128]{2,1,0:T(8,128)} %get-tuple-element.166, s32[64]{0:T(128)S(1)} %get-tuple-element.149, f32[64,128,128]{2,1,0:T(8,128)} %convolution_multiply_fusion.4), kind=kCustom, calls=%fused_computation.8.clone.1 | custom fusion | flops 1048576 | bytes 12583168 | tf_op jit(solution)/shard_map/while/body/scatter-add | solution.py:81
  162.5 4.3 gather_fusion.1
  166.8 4.6 convolution_multiply_fusion.5
  171.4 13.6 %scatter_fusion.1 = f32[64,128,128]{2,1,0:T(8,128)} fusion(f32[64,128,128]{2,1,0:T(8,128)} %get-tuple-element.167, s32[64]{0:T(128)S(1)} %get-tuple-element.150, f32[64,128,128]{2,1,0:T(8,128)} %convolution_multiply_fusion.5), kind=kCustom, calls=%fused_computation.9.clone.1 | custom fusion | flops 1048576 | bytes 12583168 | tf_op jit(solution)/shard_map/while/body/scatter-add | solution.py:81
  185.0 0.8 compare_select_fusion.8
  186.3 2.5 gather_fusion
  188.9 0.7 compare_convert_fusion.2
  189.5 4.2 convolution_multiply_fusion.4
  193.8 13.6 %scatter_fusion = f32[256,128,128]{2,1,0:T(8,128)} fusion(f32[256,128,128]{2,1,0:T(8,128)} %get-tuple-element.166, s32[64]{0:T(128)S(1)} %get-tuple-element.149, f32[64,128,128]{2,1,0:T(8,128)} %convolution_multiply_fusion.4), kind=kCustom, calls=%fused_computation.8.clone.1 | custom fusion | flops 1048576 | bytes 12583168 | tf_op jit(solution)/shard_map/while/body/scatter-add | solution.py:81
  207.4 4.3 gather_fusion.1
  211.7 4.6 convolution_multiply_fusion.5
  216.3 13.7 %scatter_fusion.1 = f32[64,128,128]{2,1,0:T(8,128)} fusion(f32[64,128,128]{2,1,0:T(8,128)} %get-tuple-element.167, s32[64]{0:T(128)S(1)} %get-tuple-element.150, f32[64,128,128]{2,1,0:T(8,128)} %convolution_multiply_fusion.5), kind=kCustom, calls=%fused_computation.9.clone.1 | custom fusion | flops 1048576 | bytes 12583168 | tf_op jit(solution)/shard_map/while/body/scatter-add | solution.py:81
  230.0 9.2 %convert_element_type.55 = bf16[256,128,128]{2,1,0:T(8,128)(2,1)} convert(f32[256,128,128]{2,1,0:T(8,128)} %get-tuple-element.57) | non-fusion elementwise | flops 4194304 | bytes 25165824 | tf_op jit(solution)/shard_map/convert_element_type | solution.py:120
  239.2 0.7 copy-done.4
  240.6 2.4 scatter_custom_fusion.2
  243.0 0.7 all_to_all.30
  243.7 232.4 %all-to-all-start.2 = ((s32[128,1,8]{2,1,0:T(1,128)}), s32[128,1,8]{2,1,0:T(1,128)S(1)}, u32[]{:S(2)}, u32[]{:S(2)}) async-start(s32[128,1,8]{2,1,0:T(1,128)} %bitcast.17), calls=%async_computation.3 | async-start | bytes 131072 | tf_op jit(solution)/shard_map/all_to_all | solution.py:134
  476.9 2.4 scatter_custom_fusion.3
  479.3 0.7 all_to_all.34
  480.0 5.6 all-to-all-done.2
  485.6 4.6 all-to-all-start.4
  490.3 4.0 convert_element_type.58
  494.2 5.7 all-to-all-done.4
  499.9 4.7 all-to-all-start.1
  504.6 0.8 compare_select_fusion.6
  505.6 25.2 %all-to-all-done.1 = bf16[8,1024,128]{2,1,0:T(8,128)(2,1)S(1)} async-done(((bf16[8,1024,128]{2,1,0:T(8,128)(2,1)}), bf16[8,1024,128]{2,1,0:T(8,128)(2,1)S(1)}, u32[]{:S(2)}, u32[]{:S(2)}) %all-to-all-start.1) | async-done | bytes 2097184 | tf_op jit(solution)/shard_map/all_to_all | solution.py:37
  531.2 4.0 gather_fusion.6
  535.2 4.4 all-to-all-start.5
  539.6 0.6 gather_fusion.4
  540.2 10.7 %all-gather = f32[32,128]{1,0:T(8,128)S(1)} all-gather(f32[8,128]{1,0:T(8,128)S(1)} %gather_fusion.4), channel_id=2, replica_groups=mesh['row_0'=4,'row_1'=2,'col_0'=4,'col_1'=4] {'row_0'}, dimensions={0}, use_global_device_ids=true | all-gather | bytes 20480 | tf_op jit(solution)/shard_map/all_gather | solution.py:44
  550.8 9.0 %all_gather.17 = f32[16,8,128]{2,1,0:T(8,128)S(1)} all-gather(f32[4,8,128]{2,1,0:T(8,128)S(1)} %bitcast.86), channel_id=1, replica_groups=mesh['row_0'=4,'row_1'=2,'col_0'=4,'col_1'=4] {'col_0'}, dimensions={0}, use_global_device_ids=true | all-gather | bytes 81920 | tf_op jit(solution)/shard_map/all_gather | solution.py:44
  559.8 10.2 %all_gather.18 = f32[64,8,128]{2,1,0:T(8,128)S(1)} all-gather(f32[16,8,128]{2,1,0:T(8,128)S(1)} %all_gather.17), channel_id=1, replica_groups=mesh['row_0'=4,'row_1'=2,'col_0'=4,'col_1'=4] {'col_1'}, dimensions={0}, use_global_device_ids=true | all-gather | bytes 327680 | tf_op jit(solution)/shard_map/all_gather | solution.py:44
  570.0 0.8 fusion.6
  570.9 1.5 fusion.4
  572.3 4.1 gather_fusion.2
  576.4 15.6 %all-to-all-start.3 = ((bf16[128,8,128]{2,1,0:T(8,128)(2,1)}), bf16[128,8,128]{2,1,0:T(8,128)(2,1)S(1)}, u32[]{:S(2)}, u32[]{:S(2)}) async-start(bf16[128,8,128]{2,1,0:T(8,128)(2,1)} %bitcast.66), calls=%async_computation.4 | async-start | bytes 524288 | tf_op jit(solution)/shard_map/all_to_all | solution.py:136
  592.1 2.9 all_gather.19
  595.0 1.0 gather_fusion.7
  596.1 6.8 %all-to-all-done.3 = bf16[128,8,128]{2,1,0:T(8,128)(2,1)S(1)} async-done(((bf16[128,8,128]{2,1,0:T(8,128)(2,1)}), bf16[128,8,128]{2,1,0:T(8,128)(2,1)S(1)}, u32[]{:S(2)}, u32[]{:S(2)}) %all-to-all-start.3) | async-done | bytes 262176 | tf_op jit(solution)/shard_map/all_to_all | solution.py:136
  603.0 1.0 gather_fusion.5
  604.0 1.3 gather_fusion.3
  605.5 3.1 exponential_log-plus-one_fusion
  (65 shorter events, 3.4 us)
Async XLA Ops:
  7.2 77.5 %all-gather.3.cloned.1.call-start = ((), (), s32[]{:S(2)}) async-start(), calls=%async_computation.7 | async-start | bytes 8912896 | tf_op jit(solution)/shard_map/all_gather | solution.py:112
  12.0 32.2 %all-to-all-start = ((bf16[8,1,1,1024,128]{4,3,2,1,0:T(8,128)(2,1)}), bf16[8,1,1,1024,128]{4,3,2,1,0:T(8,128)(2,1)S(1)}, u32[]{:S(2)}, u32[]{:S(2)}) async-start(bf16[8,1,1,1024,128]{4,3,2,1,0:T(8,128)(2,1)} %broadcast_in_dim.25), calls=%async_computation | async-start | bytes 4194304 | tf_op jit(solution)/shard_map/all_to_all | solution.py:15
  17.9 552.9 %reduce-scatter.2.cloned.1.call-start = ((), (), s32[]{:S(2)}) async-start(), calls=%async_computation.8 | async-start | bytes 8912896 | tf_op jit(solution)/shard_map/reduce_scatter | solution.py:119
  95.0 1.3 copy-start
  126.5 13.6 %copy-start.1 = (bf16[64,128,128]{2,1,0:T(8,128)(2,1)S(1)}, bf16[64,128,128]{2,1,0:T(8,128)(2,1)}, u32[]{:S(2)}) copy-start(bf16[64,128,128]{2,1,0:T(8,128)(2,1)} %copy-done) | copy-start | bytes 6291460 | tf_op jit(solution)/shard_map/while
  140.0 1.3 copy-start
  171.4 13.6 %copy-start.1 = (bf16[64,128,128]{2,1,0:T(8,128)(2,1)S(1)}, bf16[64,128,128]{2,1,0:T(8,128)(2,1)}, u32[]{:S(2)}) copy-start(bf16[64,128,128]{2,1,0:T(8,128)(2,1)} %copy-done) | copy-start | bytes 6291460 | tf_op jit(solution)/shard_map/while
  185.0 1.3 copy-start
  216.3 13.7 %copy-start.1 = (bf16[64,128,128]{2,1,0:T(8,128)(2,1)S(1)}, bf16[64,128,128]{2,1,0:T(8,128)(2,1)}, u32[]{:S(2)}) copy-start(bf16[64,128,128]{2,1,0:T(8,128)(2,1)} %copy-done) | copy-start | bytes 6291460 | tf_op jit(solution)/shard_map/while
  239.2 0.7 copy-start.4
  239.2 236.9 %copy-start.5 = (s32[512]{0:T(512)S(1)}, s32[512]{0:T(512)}, u32[]{:S(2)}) copy-start(s32[512]{0:T(512)} %param.18) | copy-start | bytes 6148
  243.7 241.9 %all-to-all-start.2 = ((s32[128,1,8]{2,1,0:T(1,128)}), s32[128,1,8]{2,1,0:T(1,128)S(1)}, u32[]{:S(2)}, u32[]{:S(2)}) async-start(s32[128,1,8]{2,1,0:T(1,128)} %bitcast.17), calls=%async_computation.3 | async-start | bytes 131072 | tf_op jit(solution)/shard_map/all_to_all | solution.py:134
  485.6 14.3 %all-to-all-start.4 = ((s32[128,1,8]{2,1,0:T(1,128)}), s32[128,1,8]{2,1,0:T(1,128)S(1)}, u32[]{:S(2)}, u32[]{:S(2)}) async-start(s32[128,1,8]{2,1,0:T(1,128)} %bitcast.30), calls=%async_computation.5 | async-start | bytes 131072 | tf_op jit(solution)/shard_map/all_to_all | solution.py:135
  494.2 36.9 %copy-start.3 = (f32[1,1,1024,128]{3,2,1,0:T(8,128)S(1)}, f32[1,1,1024,128]{3,2,1,0:T(8,128)}, u32[]{:S(2)}) copy-start(f32[1,1,1024,128]{3,2,1,0:T(8,128)} %param.12) | copy-start | bytes 1572868
  499.9 30.9 %all-to-all-start.1 = ((bf16[8,1024,128]{2,1,0:T(8,128)(2,1)}), bf16[8,1024,128]{2,1,0:T(8,128)(2,1)S(1)}, u32[]{:S(2)}, u32[]{:S(2)}) async-start(bf16[8,1024,128]{2,1,0:T(8,128)(2,1)} %bitcast.11), calls=%async_computation.2 | async-start | bytes 4194304 | tf_op jit(solution)/shard_map/all_to_all | solution.py:37
  535.2 41.2 %all-to-all-start.5 = ((bf16[128,8,128]{2,1,0:T(8,128)(2,1)}), bf16[128,8,128]{2,1,0:T(8,128)(2,1)S(1)}, u32[]{:S(2)}, u32[]{:S(2)}) async-start(bf16[128,8,128]{2,1,0:T(8,128)(2,1)} %bitcast.65), calls=%async_computation.6 | async-start | bytes 524288 | tf_op jit(solution)/shard_map/all_to_all | solution.py:143
  572.3 30.6 %copy-start.2 = (f32[2048,128]{1,0:T(8,128)}, f32[2048,128]{1,0:T(8,128)S(1)}, u32[]{:S(2)}) copy-start(f32[2048,128]{1,0:T(8,128)S(1)} %fusion.4) | copy-start | bytes 3145732
  576.4 26.5 %all-to-all-start.3 = ((bf16[128,8,128]{2,1,0:T(8,128)(2,1)}), bf16[128,8,128]{2,1,0:T(8,128)(2,1)S(1)}, u32[]{:S(2)}, u32[]{:S(2)}) async-start(bf16[128,8,128]{2,1,0:T(8,128)(2,1)} %bitcast.66), calls=%async_computation.4 | async-start | bytes 524288 | tf_op jit(solution)/shard_map/all_to_all | solution.py:136
Sparse Core Ops, SparseCore 0:
  10.7 73.9 all-gather.2
  239.3 311.7 reduce-scatter.1
where the time goes:
time: 619 us; the launch traced here: 615 us
  starting transfers between devices  268 us (43%)
  waiting for transfers between devices  109 us (18%)
  other arithmetic  107 us (17%)
  local copies, waits for them, and re-layouts  53.6 us (9%)
  blocking collectives  32.7 us (5%)
  matrix products  29.6 us (5%)
  between operations  15 us (2%)
    all_to_all x1, starting transfers between devices, on_device(): lax.all_to_all(user_request, ROW_COL, split_axis=0, concat_axis=0, tiled=...  232 us
    scatter-add x3, other arithmetic, advance(): user_part.at[row_ids].add(to_users)  41 us
    scatter-add x3, other arithmetic, advance(): item_part.at[col_ids].add(to_items)  40.8 us
    all_gather x1, waiting for transfers between devices, on_device(): lax.all_gather(user_emb.astype(jnp.bfloat16), COL, axis=1, tiled=True)  40.6 us
    all_gather x4, blocking collectives, gather_in_order(): blocks = lax.all_gather(blocks, axes[k], axis=0, tiled=True)  32.7 us
    all_to_all x1, waiting for transfers between devices, from_everyone(): return lax.all_to_all(copies, axis, split_axis=0, concat_axis=0, tiled=True)  25.5 us
    all_to_all x1, waiting for transfers between devices, sent_and_summed(): lax.all_to_all(blocks, axis, split_axis=0, concat_axis=0, tiled=True)  25.2 us
    all_to_all x1, starting transfers between devices, on_device(): lax.all_to_all(user_final[user_wanted].astype(jnp.bfloat16), ROW_COL, spl...  15.6 us
  transfers between devices with their start and end apart: 8, of which 6 were waited for; matrix products, arithmetic and copies ran while one was open for 4% of the time, Pallas kernels for 0%

commit v1 on v0

--- a/solution.py
+++ b/solution.py
@@ -109,7 +109,11 @@
     item_dev = item_emb.shape[2]
     embed = user_emb.shape[3]
     tile_side = tile_vals.shape[-1]
-    user_whole = lax.all_gather(user_emb.astype(jnp.bfloat16), COL, axis=1, tiled=True)
+    block = user_emb.astype(jnp.bfloat16)
+    size = lax.axis_size(COL)
+    parts = jnp.stack([block for _ in range(size)])
+    parts = lax.all_to_all(parts, COL, split_axis=0, concat_axis=0)
+    user_whole = jnp.concatenate(parts, axis=1)
     item_whole = collect(item_emb.astype(jnp.bfloat16), ROW, 1)
     user_tiles = user_whole.reshape(-1, tile_side, embed)
     item_tiles = item_whole.reshape(-1, tile_side, embed)

time: 619 us -> 738 us (1.19)
  waiting for transfers between devices: 109 us -> 210 us
  starting transfers between devices: 268 us -> 280 us
    all_to_all x0 -> x1, waiting for transfers between devices: none -> 142 us  [on_device(): parts = lax.all_to_all(parts, COL, split_axis=0, concat_axis=0)]
    all_gather x1 -> x0, waiting for transfers between devices: 40.6 us -> none  [on_device(): lax.all_gather(user_emb.astype(jnp.bfloat16), COL, axis=1, tiled=True)]
    all_to_all x0 -> x1, starting transfers between devices: none -> 7.65 us  [on_device(): parts = lax.all_to_all(parts, COL, split_axis=0, concat_axis=0)]
  transfers between devices with their start and end apart: 8 -> 8, of which waited for: 6 -> 6; matrix products, arithmetic and copies ran while one was open for 4% -> 3% of each run, Pallas kernels for 0% -> 0%
where the time goes in v1:
time: 738 us; the launch traced here: 734 us
  starting transfers between devices  280 us (38%)
  waiting for transfers between devices  210 us (28%)
  other arithmetic  106 us (14%)
  local copies, waits for them, and re-layouts  59.5 us (8%)
  blocking collectives  32.7 us (4%)
  matrix products  29.6 us (4%)
  between operations  15 us (2%)
    all_to_all x1, starting transfers between devices, on_device(): lax.all_to_all(user_request, ROW_COL, split_axis=0, concat_axis=0, tiled=...  238 us
    all_to_all x1, waiting for transfers between devices, on_device(): parts = lax.all_to_all(parts, COL, split_axis=0, concat_axis=0)  142 us
    scatter-add x3, other arithmetic, advance(): user_part.at[row_ids].add(to_users)  41 us
    scatter-add x3, other arithmetic, advance(): item_part.at[col_ids].add(to_items)  40.8 us
    all_gather x4, blocking collectives, gather_in_order(): blocks = lax.all_gather(blocks, axes[k], axis=0, tiled=True)  32.7 us
    all_to_all x1, waiting for transfers between devices, from_everyone(): return lax.all_to_all(copies, axis, split_axis=0, concat_axis=0, tiled=True)  25.4 us
    all_to_all x1, waiting for transfers between devices, sent_and_summed(): lax.all_to_all(blocks, axis, split_axis=0, concat_axis=0, tiled=True)  25.2 us
    all_to_all x1, starting transfers between devices, on_device(): lax.all_to_all(user_final[user_wanted].astype(jnp.bfloat16), ROW_COL, spl...  15.7 us
  transfers between devices with their start and end apart: 8, of which 6 were waited for; matrix products, arithmetic and copies ran while one was open for 3% of the time, Pallas kernels for 0%

profile of v1, /device:TPU:1, one launch (start us, length us, event | category | flops | bytes accessed | tf_op | source)
XLA Modules:
  0.0 733.8 jit_solution(10728154804819847810)
XLA Ops:
  7.2 1.2 convert_bitcast_fusion.3
  8.3 1.6 broadcast_in_dim.25
  9.9 6.0 all-to-all-start
  15.9 0.8 convert_bitcast_fusion
  16.7 25.4 %all-to-all-done = bf16[8,1,1,1024,128]{4,3,2,1,0:T(8,128)(2,1)S(1)} async-done(((bf16[8,1,1,1024,128]{4,3,2,1,0:T(8,128)(2,1)}), bf16[8,1,1,1024,128]{4,3,2,1,0:T(8,128)(2,1)S(1)}, u32[]{:S(2)}, u32[]{:S(2)}) %all-to-all-start) | async-done | bytes 2097184 | tf_op jit(solution)/shard_map/all_to_all | solution.py:15
  42.1 5.9 stack.2
  48.0 7.6 %all-to-all-start.1 = ((bf16[16,1,1,2048,128]{4,3,2,1,0:T(8,128)(2,1)}), bf16[16,1,1,2048,128]{4,3,2,1,0:T(8,128)(2,1)}, u32[]{:S(2)}, u32[]{:S(2)}) async-start(bf16[16,1,1,2048,128]{4,3,2,1,0:T(8,128)(2,1)} %stack.2), calls=%async_computation.1 | async-start | bytes 16777216 | tf_op jit(solution)/shard_map/all_to_all | solution.py:115
  56.3 141.6 %all-to-all-done.1 = bf16[16,1,1,2048,128]{4,3,2,1,0:T(8,128)(2,1)} async-done(((bf16[16,1,1,2048,128]{4,3,2,1,0:T(8,128)(2,1)}), bf16[16,1,1,2048,128]{4,3,2,1,0:T(8,128)(2,1)}, u32[]{:S(2)}, u32[]{:S(2)}) %all-to-all-start.1) | async-done | bytes 8388640 | tf_op jit(solution)/shard_map/all_to_all | solution.py:115
  197.9 7.8 %broadcast_in_dim.23 = f32[256,128,128]{2,1,0:T(8,128)} broadcast(f32[]{:T(128)} %constant.123.clone.1), dimensions={} | broadcast | bytes 16777220 | tf_op jit(solution)/shard_map/broadcast_in_dim | solution.py:83
  205.8 2.5 broadcast_in_dim.24
  208.3 135.0 %while.12 = (s32[]{:T(128)}, f32[256,128,128]{2,1,0:T(8,128)}, f32[64,128,128]{2,1,0:T(8,128)}, s32[]{:T(128)}, s32[512]{0:T(512)}, /*index=5*/bf16[512,128,128]...) while((s32[]{:T(128)}, f32[256,128,128]{2,1,0:T(8,128)}, ...), condition=%wide.region_3.4_spmd, body=%wide.region_0.3_spmd.sunk | while | flops 541067840 | bytes 67120640 | solution.py:84
  208.3 0.8 compare_select_fusion.8
  209.6 2.5 gather_fusion
  212.1 0.7 compare_convert_fusion.2
  212.8 4.2 convolution_multiply_fusion.4
  217.0 13.7 %scatter_fusion = f32[256,128,128]{2,1,0:T(8,128)} fusion(f32[256,128,128]{2,1,0:T(8,128)} %get-tuple-element.166, s32[64]{0:T(128)S(1)} %get-tuple-element.149, f32[64,128,128]{2,1,0:T(8,128)} %convolution_multiply_fusion.4), kind=kCustom, calls=%fused_computation.8.clone.1 | custom fusion | flops 1048576 | bytes 12583168 | tf_op jit(solution)/shard_map/while/body/scatter-add | solution.py:81
  230.8 4.3 gather_fusion.1
  235.1 4.6 convolution_multiply_fusion.5
  239.7 13.6 %scatter_fusion.1 = f32[64,128,128]{2,1,0:T(8,128)} fusion(f32[64,128,128]{2,1,0:T(8,128)} %get-tuple-element.167, s32[64]{0:T(128)S(1)} %get-tuple-element.150, f32[64,128,128]{2,1,0:T(8,128)} %convolution_multiply_fusion.5), kind=kCustom, calls=%fused_computation.9.clone.1 | custom fusion | flops 1048576 | bytes 12583168 | tf_op jit(solution)/shard_map/while/body/scatter-add | solution.py:81
  253.3 0.8 compare_select_fusion.8
  254.6 2.5 gather_fusion
  257.1 0.7 compare_convert_fusion.2
  257.8 4.2 convolution_multiply_fusion.4
  262.0 13.6 %scatter_fusion = f32[256,128,128]{2,1,0:T(8,128)} fusion(f32[256,128,128]{2,1,0:T(8,128)} %get-tuple-element.166, s32[64]{0:T(128)S(1)} %get-tuple-element.149, f32[64,128,128]{2,1,0:T(8,128)} %convolution_multiply_fusion.4), kind=kCustom, calls=%fused_computation.8.clone.1 | custom fusion | flops 1048576 | bytes 12583168 | tf_op jit(solution)/shard_map/while/body/scatter-add | solution.py:81
  275.7 4.3 gather_fusion.1
  280.0 4.6 convolution_multiply_fusion.5
  284.6 13.6 %scatter_fusion.1 = f32[64,128,128]{2,1,0:T(8,128)} fusion(f32[64,128,128]{2,1,0:T(8,128)} %get-tuple-element.167, s32[64]{0:T(128)S(1)} %get-tuple-element.150, f32[64,128,128]{2,1,0:T(8,128)} %convolution_multiply_fusion.5), kind=kCustom, calls=%fused_computation.9.clone.1 | custom fusion | flops 1048576 | bytes 12583168 | tf_op jit(solution)/shard_map/while/body/scatter-add | solution.py:81
  298.2 0.8 compare_select_fusion.8
  299.6 2.5 gather_fusion
  302.1 0.7 compare_convert_fusion.2
  302.8 4.2 convolution_multiply_fusion.4
  307.0 13.6 %scatter_fusion = f32[256,128,128]{2,1,0:T(8,128)} fusion(f32[256,128,128]{2,1,0:T(8,128)} %get-tuple-element.166, s32[64]{0:T(128)S(1)} %get-tuple-element.149, f32[64,128,128]{2,1,0:T(8,128)} %convolution_multiply_fusion.4), kind=kCustom, calls=%fused_computation.8.clone.1 | custom fusion | flops 1048576 | bytes 12583168 | tf_op jit(solution)/shard_map/while/body/scatter-add | solution.py:81
  320.6 4.3 gather_fusion.1
  325.0 4.6 convolution_multiply_fusion.5
  329.6 13.7 %scatter_fusion.1 = f32[64,128,128]{2,1,0:T(8,128)} fusion(f32[64,128,128]{2,1,0:T(8,128)} %get-tuple-element.167, s32[64]{0:T(128)S(1)} %get-tuple-element.150, f32[64,128,128]{2,1,0:T(8,128)} %convolution_multiply_fusion.5), kind=kCustom, calls=%fused_computation.9.clone.1 | custom fusion | flops 1048576 | bytes 12583168 | tf_op jit(solution)/shard_map/while/body/scatter-add | solution.py:81
  343.2 9.2 %convert_element_type.58 = bf16[256,128,128]{2,1,0:T(8,128)(2,1)} convert(f32[256,128,128]{2,1,0:T(8,128)} %get-tuple-element.57) | non-fusion elementwise | flops 4194304 | bytes 25165824 | tf_op jit(solution)/shard_map/convert_element_type | solution.py:124
  352.4 0.7 copy-done.5
  353.8 2.4 scatter_custom_fusion.2
  356.3 0.7 all_to_all.34
  357.0 237.5 %all-to-all-start.3 = ((s32[128,1,8]{2,1,0:T(1,128)}), s32[128,1,8]{2,1,0:T(1,128)S(1)}, u32[]{:S(2)}, u32[]{:S(2)}) async-start(s32[128,1,8]{2,1,0:T(1,128)} %bitcast.17), calls=%async_computation.4 | async-start | bytes 131072 | tf_op jit(solution)/shard_map/all_to_all | solution.py:138
  595.3 2.4 scatter_custom_fusion.3
  597.7 0.7 all_to_all.38
  598.4 5.6 all-to-all-done.3
  604.0 4.6 all-to-all-start.5
  608.6 4.0 convert_element_type.61
  612.6 5.7 all-to-all-done.5
  618.3 4.7 all-to-all-start.2
  623.0 0.8 compare_select_fusion.6
  624.0 25.2 %all-to-all-done.2 = bf16[8,1024,128]{2,1,0:T(8,128)(2,1)S(1)} async-done(((bf16[8,1024,128]{2,1,0:T(8,128)(2,1)}), bf16[8,1024,128]{2,1,0:T(8,128)(2,1)S(1)}, u32[]{:S(2)}, u32[]{:S(2)}) %all-to-all-start.2) | async-done | bytes 2097184 | tf_op jit(solution)/shard_map/all_to_all | solution.py:37
  649.6 4.0 gather_fusion.6
  653.6 4.4 all-to-all-start.6
  658.6 10.7 %all-gather = f32[32,128]{1,0:T(8,128)S(1)} all-gather(f32[8,128]{1,0:T(8,128)S(1)} %gather_fusion.4), channel_id=2, replica_groups=mesh['row_0'=4,'row_1'=2,'col_0'=4,'col_1'=4] {'row_0'}, dimensions={0}, use_global_device_ids=true | all-gather | bytes 20480 | tf_op jit(solution)/shard_map/all_gather | solution.py:44
  669.2 9.1 %all_gather.13 = f32[16,8,128]{2,1,0:T(8,128)S(1)} all-gather(f32[4,8,128]{2,1,0:T(8,128)S(1)} %bitcast.85), channel_id=1, replica_groups=mesh['row_0'=4,'row_1'=2,'col_0'=4,'col_1'=4] {'col_0'}, dimensions={0}, use_global_device_ids=true | all-gather | bytes 81920 | tf_op jit(solution)/shard_map/all_gather | solution.py:44
  678.3 10.1 %all_gather.14 = f32[64,8,128]{2,1,0:T(8,128)S(1)} all-gather(f32[16,8,128]{2,1,0:T(8,128)S(1)} %all_gather.13), channel_id=1, replica_groups=mesh['row_0'=4,'row_1'=2,'col_0'=4,'col_1'=4] {'col_1'}, dimensions={0}, use_global_device_ids=true | all-gather | bytes 327680 | tf_op jit(solution)/shard_map/all_gather | solution.py:44
  688.4 0.8 fusion.6
  689.3 1.5 fusion.4
  690.7 4.1 gather_fusion.2
  694.8 15.7 %all-to-all-start.4 = ((bf16[128,8,128]{2,1,0:T(8,128)(2,1)}), bf16[128,8,128]{2,1,0:T(8,128)(2,1)S(1)}, u32[]{:S(2)}, u32[]{:S(2)}) async-start(bf16[128,8,128]{2,1,0:T(8,128)(2,1)} %bitcast.66), calls=%async_computation.5 | async-start | bytes 524288 | tf_op jit(solution)/shard_map/all_to_all | solution.py:140
  710.5 2.9 all_gather.15
  713.5 1.0 gather_fusion.7
  714.5 6.8 all-to-all-done.4
  721.4 1.0 gather_fusion.5
  722.4 1.3 gather_fusion.3
  723.9 3.1 exponential_log-plus-one_fusion
  (67 shorter events, 4.4 us)
Async XLA Ops:
  7.2 8.7 %copy-start.4 = (f32[1,1,2048,128]{3,2,1,0:T(8,128)S(1)}, f32[1,1,2048,128]{3,2,1,0:T(8,128)}, u32[]{:S(2)}) copy-start(f32[1,1,2048,128]{3,2,1,0:T(8,128)} %param.11) | copy-start | bytes 3145732
  9.9 32.2 %all-to-all-start = ((bf16[8,1,1,1024,128]{4,3,2,1,0:T(8,128)(2,1)}), bf16[8,1,1,1024,128]{4,3,2,1,0:T(8,128)(2,1)S(1)}, u32[]{:S(2)}, u32[]{:S(2)}) async-start(bf16[8,1,1,1024,128]{4,3,2,1,0:T(8,128)(2,1)} %broadcast_in_dim.25), calls=%async_computation | async-start | bytes 4194304 | tf_op jit(solution)/shard_map/all_to_all | solution.py:15
  48.0 149.9 %all-to-all-start.1 = ((bf16[16,1,1,2048,128]{4,3,2,1,0:T(8,128)(2,1)}), bf16[16,1,1,2048,128]{4,3,2,1,0:T(8,128)(2,1)}, u32[]{:S(2)}, u32[]{:S(2)}) async-start(bf16[16,1,1,2048,128]{4,3,2,1,0:T(8,128)(2,1)} %stack.2), calls=%async_computation.1 | async-start | bytes 16777216 | tf_op jit(solution)/shard_map/all_to_all | solution.py:115
  55.6 633.6 %reduce-scatter.2.cloned.1.call-start = ((), (), s32[]{:S(2)}) async-start(), calls=%async_computation.8 | async-start | bytes 8912896 | tf_op jit(solution)/shard_map/reduce_scatter | solution.py:123
  208.3 1.3 copy-start
  239.7 13.6 %copy-start.1 = (bf16[64,128,128]{2,1,0:T(8,128)(2,1)S(1)}, bf16[64,128,128]{2,1,0:T(8,128)(2,1)}, u32[]{:S(2)}) copy-start(bf16[64,128,128]{2,1,0:T(8,128)(2,1)} %copy-done) | copy-start | bytes 6291460 | tf_op jit(solution)/shard_map/while
  253.3 1.3 copy-start
  284.6 13.6 %copy-start.1 = (bf16[64,128,128]{2,1,0:T(8,128)(2,1)S(1)}, bf16[64,128,128]{2,1,0:T(8,128)(2,1)}, u32[]{:S(2)}) copy-start(bf16[64,128,128]{2,1,0:T(8,128)(2,1)} %copy-done) | copy-start | bytes 6291460 | tf_op jit(solution)/shard_map/while
  298.2 1.3 copy-start
  329.6 13.7 %copy-start.1 = (bf16[64,128,128]{2,1,0:T(8,128)(2,1)S(1)}, bf16[64,128,128]{2,1,0:T(8,128)(2,1)}, u32[]{:S(2)}) copy-start(bf16[64,128,128]{2,1,0:T(8,128)(2,1)} %copy-done) | copy-start | bytes 6291460 | tf_op jit(solution)/shard_map/while
  352.4 0.7 copy-start.5
  352.4 242.1 %copy-start.6 = (s32[512]{0:T(512)S(1)}, s32[512]{0:T(512)}, u32[]{:S(2)}) copy-start(s32[512]{0:T(512)} %param.18) | copy-start | bytes 6148
  357.0 247.1 %all-to-all-start.3 = ((s32[128,1,8]{2,1,0:T(1,128)}), s32[128,1,8]{2,1,0:T(1,128)S(1)}, u32[]{:S(2)}, u32[]{:S(2)}) async-start(s32[128,1,8]{2,1,0:T(1,128)} %bitcast.17), calls=%async_computation.4 | async-start | bytes 131072 | tf_op jit(solution)/shard_map/all_to_all | solution.py:138
  604.0 14.3 %all-to-all-start.5 = ((s32[128,1,8]{2,1,0:T(1,128)}), s32[128,1,8]{2,1,0:T(1,128)S(1)}, u32[]{:S(2)}, u32[]{:S(2)}) async-start(s32[128,1,8]{2,1,0:T(1,128)} %bitcast.30), calls=%async_computation.6 | async-start | bytes 131072 | tf_op jit(solution)/shard_map/all_to_all | solution.py:139
  612.6 36.9 %copy-start.3 = (f32[1,1,1024,128]{3,2,1,0:T(8,128)S(1)}, f32[1,1,1024,128]{3,2,1,0:T(8,128)}, u32[]{:S(2)}) copy-start(f32[1,1,1024,128]{3,2,1,0:T(8,128)} %param.12) | copy-start | bytes 1572868
  618.3 30.9 %all-to-all-start.2 = ((bf16[8,1024,128]{2,1,0:T(8,128)(2,1)}), bf16[8,1024,128]{2,1,0:T(8,128)(2,1)S(1)}, u32[]{:S(2)}, u32[]{:S(2)}) async-start(bf16[8,1024,128]{2,1,0:T(8,128)(2,1)} %bitcast.11), calls=%async_computation.3 | async-start | bytes 4194304 | tf_op jit(solution)/shard_map/all_to_all | solution.py:37
  653.6 41.2 %all-to-all-start.6 = ((bf16[128,8,128]{2,1,0:T(8,128)(2,1)}), bf16[128,8,128]{2,1,0:T(8,128)(2,1)S(1)}, u32[]{:S(2)}, u32[]{:S(2)}) async-start(bf16[128,8,128]{2,1,0:T(8,128)(2,1)} %bitcast.65), calls=%async_computation.7 | async-start | bytes 524288 | tf_op jit(solution)/shard_map/all_to_all | solution.py:147
  690.7 30.7 %copy-start.2 = (f32[2048,128]{1,0:T(8,128)}, f32[2048,128]{1,0:T(8,128)S(1)}, u32[]{:S(2)}) copy-start(f32[2048,128]{1,0:T(8,128)S(1)} %fusion.4) | copy-start | bytes 3145732
  694.8 26.5 %all-to-all-start.4 = ((bf16[128,8,128]{2,1,0:T(8,128)(2,1)}), bf16[128,8,128]{2,1,0:T(8,128)(2,1)S(1)}, u32[]{:S(2)}, u32[]{:S(2)}) async-start(bf16[128,8,128]{2,1,0:T(8,128)(2,1)} %bitcast.66), calls=%async_computation.5 | async-start | bytes 524288 | tf_op jit(solution)/shard_map/all_to_all | solution.py:140
Sparse Core Ops, SparseCore 0:
  352.6 316.8 reduce-scatter.1
